TPU v7x, 32 devices: a whole 2x2x4 slice. The times are simulated.
32 devices in a mesh: grp: 8 (over y, x, core), loc: 4 (over z).
Axes of the slice: x: 2, y: 2, z: 4, core: 2. Of those that a mesh axis runs over, the one named last changes fastest.
Arguments:
- element_values: float32 [8, 442368], P(None, ('grp', 'loc')), may hold values from -6 to 6
- local_map: int32 [442368], P(('grp', 'loc')), may hold values from 0 to 10647, as said below
- send_node: int32 [32, 3072], P(('grp', 'loc')), may hold values from 0 to 10647, as said below
- send_count: int32 [32, 12], P(('grp', 'loc')), may hold values from 0 to 256, as said below
- recv_slot: int32 [32, 3072], P(('grp', 'loc')), may hold values from 0 to 511, as said below
Outputs:
- summed: float32 [8, 442368], P(None, ('grp', 'loc'))
Inputs may be any that keep to these rules, and one draw needn't show every extreme that they name: `local_map`: each device's block lists the nodes of its elements as points of a grid of 22 x 22 x 22 distinct nodes, elements in some order, the grid points numbered in an arbitrary order of the device's own; every number below 10648 appears in each block. `send_node`: the live slots toward one peer name distinct nodes; slots at or past a pair's count hold arbitrary node numbers. `send_count`: counts are zero toward groups past the ends of grp (no wrap), exactly 256 toward the device itself, and between 64 and 256 toward every other peer. `recv_slot`: the live slots from one sender to one owner name distinct owned nodes.
All inputs are finite; a program needn't handle non-finite values.
Results may differ from a plain program's by a relative error of at most 0.0003.
Values sent between devices are 32-bit elements; how exact they have to be, the bound alone decides.
A program may use at most 64 MiB of HBM per device.

v0:
```python
import jax
import jax.numpy as jnp
from jax import lax
from jax.sharding import PartitionSpec as P

LOCAL = 10648


def shifted(block, axis, distance):
    devices = range(lax.axis_size(axis))
    route = [(i - distance, i) for i in devices if i - distance in devices]
    return lax.ppermute(block, axis, route)


def within_inward(buffer):
    return lax.all_to_all(buffer, "loc", split_axis=2, concat_axis=2, tiled=True)


def across_inward(buffer):
    lower = shifted(buffer[:, 0], "grp", -1)
    upper = shifted(buffer[:, 2], "grp", 1)
    return jnp.stack([lower, buffer[:, 1], upper], axis=1)


def within_outward(buffer):
    return lax.all_to_all(buffer, "loc", split_axis=2, concat_axis=2, tiled=True)


def across_outward(buffer):
    lower = shifted(buffer[:, 0], "grp", 1)
    upper = shifted(buffer[:, 2], "grp", -1)
    return jnp.stack([lower, buffer[:, 1], upper], axis=1)


def on_device(element_values, local_map, send_node, send_count, recv_slot):
    fields = element_values.shape[0]
    loc_count = lax.axis_size("loc")
    slot_count = send_node.shape[1] // (3 * loc_count)
    owned_count = 2 * slot_count
    assembled = jnp.zeros((fields, LOCAL), jnp.float32).at[:, local_map].add(element_values)
    live_slot = (jnp.arange(slot_count)[None, :] < send_count[0][:, None]).reshape(-1)
    picked = jnp.where(live_slot[None, :], jnp.take(assembled, send_node[0], axis=1), 0.0)
    outgoing = picked.reshape(fields, 3, loc_count, slot_count)
    arrived = within_inward(across_inward(outgoing))
    incoming = arrived.reshape(fields, -1)
    targets = recv_slot[0]
    totals = jnp.zeros((fields, owned_count), jnp.float32).at[:, targets].add(incoming)
    replies = jnp.take(totals, targets, axis=1).reshape(fields, 3, loc_count, slot_count)
    homeward = across_outward(within_outward(replies))
    returned = homeward.reshape(fields, -1)
    change = jnp.where(live_slot[None, :], returned - picked, 0.0)
    combined = assembled.at[:, send_node[0]].add(change)
    return jnp.take(combined, local_map, axis=1)


def solution(mesh):
    return jax.shard_map(
        on_device,
        mesh=mesh,
        in_specs=(
            P(None, ("grp", "loc")),
            P(("grp", "loc")),
            P(("grp", "loc"), None),
            P(("grp", "loc"), None),
            P(("grp", "loc"), None),
        ),
        out_specs=P(None, ("grp", "loc")),
        check_vma=False,
    )
```

profile of v0, /device:TPU:12, one launch (start us, length us, event | category | flops | bytes accessed | tf_op | source)
XLA Modules:
  0.0 231.5 jit_solution(4545416513753888741)
XLA Ops:
  0.0 0.8 compare_select_fusion
  0.8 5.1 %copy.42 = f32[13824,8]{1,0:T(8,128)} copy(f32[13824,8]{0,1:T(8,128)} %bitcast.52) | data formatting | bytes 884736 | tf_op args[0]
  6.0 76.8 %scatter_custom_fusion = f32[8,10648]{0,1:T(8,128)} fusion(s32[13824]{0:T(1024)S(1)} %compare_select_fusion, f32[13824,8]{1,0:T(8,128)} %copy.42, f32[]{:T(128)} %constant.33.clone.1), kind=kCustom, calls=%fused_computation.7 | custom fusion | flops 110592 | bytes 341248 | tf_op jit(solution)/shard_map/scatter-add | solution.py:40
  82.8 10.7 %gather_fusion = f32[3072,8]{1,0:T(8,128)S(1)} fusion(f32[8,10648]{0,1:T(8,128)} %scatter_custom_fusion, s32[3072]{0:T(1024)S(1)} %broadcast_clamp_fusion.1), kind=kCustom, calls=%fused_computation | custom fusion | bytes 208896 | tf_op jit(solution)/shard_map/jit(_take)/gather | solution.py:42
  93.5 0.4 copy.43
  93.9 0.5 broadcast.116
  94.4 0.7 reduce.9
  95.1 0.7 reduce.10
  95.8 0.1 lt.92
  96.0 1.9 collective-permute-start.1
  97.9 4.5 %collective-permute-start = (f32[8,4,256]{2,0,1:T(8,128)S(1)}, f32[8,4,256]{2,0,1:T(8,128)S(1)}, u32[]{:S(2)}, u32[]{:S(2)}) collective-permute-start(f32[8,4,256]{2,0,1:T(8,128)S(1)} %get-tuple-element.8), channel_id=1, source_target_pairs={{4,0},{8,4},{12,8},{16,12},{20,16},{24,20},{28,24},{5,1},{9,5},{13... | collective-permute-start | bytes 98312 | tf_op jit(solution)/shard_map/ppermute | solution.py:12
  102.6 0.7 reduce.11
  103.3 0.8 collective-permute-done
  104.0 0.6 pad_maximum_fusion
  104.7 5.3 %all-to-all-start = ((f32[8,3,4,256]{3,0,1,2:T(8,128)}), f32[8,3,4,256]{3,0,1,2:T(8,128)S(1)}, u32[]{:S(2)}, u32[]{:S(2)}) async-start(f32[8,3,4,256]{3,0,1,2:T(8,128)} %pad_maximum_fusion), calls=%async_computation | async-start | bytes 196608 | tf_op jit(solution)/shard_map/all_to_all | solution.py:16
  110.0 5.1 %all-to-all-done = f32[8,3,4,256]{3,0,1,2:T(8,128)S(1)} async-done(((f32[8,3,4,256]{3,0,1,2:T(8,128)}), f32[8,3,4,256]{3,0,1,2:T(8,128)S(1)}, u32[]{:S(2)}, u32[]{:S(2)}) %all-to-all-start) | async-done | bytes 98336 | tf_op jit(solution)/shard_map/all_to_all | solution.py:16
  115.3 0.5 copy.47
  115.7 17.0 %scatter_custom_fusion.1 = f32[8,512]{0,1:T(8,128)S(1)} fusion(s32[3072]{0:T(1024)S(1)} %bitcast.58, f32[3072,8]{1,0:T(8,128)S(1)} %copy.47, f32[]{:T(128)} %constant.33.clone.1), kind=kCustom, calls=%fused_computation.16 | custom fusion | flops 24576 | bytes 16388 | tf_op jit(solution)/shard_map/scatter-add | solution.py:47
  132.7 8.1 %gather_fusion.1 = f32[3072,8]{1,0:T(8,128)S(1)} fusion(f32[8,512]{0,1:T(8,128)S(1)} %scatter_custom_fusion.1, s32[3072]{0:T(1024)S(1)} %broadcast_clamp_fusion), kind=kCustom, calls=%fused_computation.1 | custom fusion | bytes 208896 | tf_op jit(solution)/shard_map/jit(_take)/gather | solution.py:48
  140.8 0.4 copy.48
  141.3 0.6 copy.49
  142.0 4.2 %all-to-all-start.1 = ((f32[8,3,4,256]{3,0,1,2:T(8,128)}), f32[8,3,4,256]{3,0,1,2:T(8,128)S(1)}, u32[]{:S(2)}, u32[]{:S(2)}) async-start(f32[8,3,4,256]{3,0,1,2:T(8,128)} %copy.49), calls=%async_computation.1 | async-start | bytes 196608 | tf_op jit(solution)/shard_map/all_to_all | solution.py:26
  146.2 4.9 %all-to-all-done.1 = f32[8,3,4,256]{3,0,1,2:T(8,128)S(1)} async-done(((f32[8,3,4,256]{3,0,1,2:T(8,128)}), f32[8,3,4,256]{3,0,1,2:T(8,128)S(1)}, u32[]{:S(2)}, u32[]{:S(2)}) %all-to-all-start.1) | async-done | bytes 98336 | tf_op jit(solution)/shard_map/all_to_all | solution.py:26
  151.1 2.6 %collective-permute-start.3 = (f32[8,4,256]{2,0,1:T(8,128)S(1)}, f32[8,4,256]{2,0,1:T(8,128)S(1)}, u32[]{:S(2)}, u32[]{:S(2)}) collective-permute-start(f32[8,4,256]{2,0,1:T(8,128)S(1)} %get-tuple-element.6), channel_id=1, source_target_pairs={{4,0},{8,4},{12,8},{16,12},{20,16},{24,20},{28,24},{5,1},{9,5},{13... | collective-permute-start | bytes 98312 | tf_op jit(solution)/shard_map/ppermute | solution.py:12
  153.7 1.9 collective-permute-start.2
  155.7 4.1 %collective-permute-done.2 = f32[8,4,256]{2,0,1:T(8,128)S(1)} collective-permute-done((f32[8,4,256]{2,0,1:T(8,128)S(1)}, f32[8,4,256]{2,0,1:T(8,128)S(1)}, u32[]{:S(2)}, u32[]{:S(2)}) %collective-permute-start.2) | collective-permute-done | bytes 32800 | tf_op jit(solution)/shard_map/ppermute | solution.py:12
  159.8 1.6 copy.52
  161.5 4.2 %fusion.4 = f32[8,3072]{0,1:T(8,128)S(1)} fusion(f32[8,3,4,256]{0,3,2,1:T(8,128)} %copy.52, f32[3072,8]{1,0:T(8,128)S(1)} %gather_fusion, pred[3072]{0:T(1024)(128)(4,1)S(1)} %compare_and_fusion.1, pred[3072]{0:T(1024)(128)(4,1)S(1)} %lt.88), kind=kLoop, calls=%fused_computation.12 | loop fusion | flops 98304 | bytes 301056 | tf_op jit(solution)/shard_map/jit(_where)/select_n | solution.py:51
  165.7 20.2 %scatter_custom_fusion.2 = f32[8,10648]{0,1:T(8,128)} fusion(f32[8,10648]{0,1:T(8,128)} %scatter_custom_fusion, s32[3072]{0:T(1024)S(1)} %bitcast.56, f32[8,3072]{0,1:T(8,128)S(1)} %fusion.4), kind=kCustom, calls=%fused_computation.9 | custom fusion | flops 24576 | bytes 1913600 | tf_op jit(solution)/shard_map/scatter-add | solution.py:52
  185.9 28.6 %gather_fusion.2 = f32[13824,8]{1,0:T(8,128)} fusion(f32[8,10648]{0,1:T(8,128)} %scatter_custom_fusion.2, s32[14336]{0:T(1024)S(1)} %pad_clamp_fusion), kind=kCustom, calls=%fused_computation.2 | custom fusion | bytes 940032 | tf_op jit(solution)/shard_map/jit(_take)/gather | solution.py:53
  214.5 11.6 %select_bitcast_fusion = f32[8,13824]{0,1:T(8,128)} fusion(f32[13824,8]{1,0:T(8,128)} %gather_fusion.2, pred[13824]{0:T(1024)(128)(4,1)S(1)} %compare_and_fusion), kind=kLoop, calls=%fused_computation.6 | loop fusion | flops 110592 | bytes 898560 | tf_op jit(solution)/shard_map/jit(_take)/select_n | solution.py:53
  226.1 5.4 %copy.53 = f32[8,13824]{1,0:T(8,128)} copy(f32[8,13824]{0,1:T(8,128)} %select_bitcast_fusion) | data formatting | bytes 884736 | tf_op jit(solution)/shard_map/jit(_take)/select_n | solution.py:53
  (30 shorter events, 0.5 us)
Async XLA Ops:
  0.8 5.1 %copy-start.1 = (s32[1,3072]{1,0:T(1,128)S(1)}, s32[1,3072]{1,0:T(1,128)}, u32[]{:S(2)}) copy-start(s32[1,3072]{1,0:T(1,128)} %param.7) | copy-start | bytes 36868
  82.8 12.3 %copy-start.3 = (s32[1,12]{1,0:T(1,128)S(1)}, s32[1,12]{1,0:T(1,128)}, u32[]{:S(2)}) copy-start(s32[1,12]{1,0:T(1,128)} %param.8) | copy-start | bytes 148
  82.8 19.7 %copy-start = (s32[13824]{0:T(1024)S(1)}, s32[13824]{0:T(1024)}, u32[]{:S(2)}) copy-start(s32[13824]{0:T(1024)} %param.6) | copy-start | bytes 165892
  82.8 19.8 %copy-start.2 = (s32[1,3072]{1,0:T(1,128)S(1)}, s32[1,3072]{1,0:T(1,128)}, u32[]{:S(2)}) copy-start(s32[1,3072]{1,0:T(1,128)} %param.9) | copy-start | bytes 36868
  96.0 7.3 %collective-permute-start.1 = (f32[8,4,256]{2,0,1:T(8,128)S(1)}, f32[8,4,256]{2,0,1:T(8,128)S(1)}, u32[]{:S(2)}, u32[]{:S(2)}) collective-permute-start(f32[8,4,256]{2,0,1:T(8,128)S(1)} %get-tuple-element.9), channel_id=1, source_target_pairs={{0,4},{4,8},{8,12},{12,16},{16,20},{20,24},{24,28},{1,5},{5,9},{9,... | collective-permute-start | bytes 98312 | tf_op jit(solution)/shard_map/ppermute | solution.py:12
  97.9 6.1 %collective-permute-start = (f32[8,4,256]{2,0,1:T(8,128)S(1)}, f32[8,4,256]{2,0,1:T(8,128)S(1)}, u32[]{:S(2)}, u32[]{:S(2)}) collective-permute-start(f32[8,4,256]{2,0,1:T(8,128)S(1)} %get-tuple-element.8), channel_id=1, source_target_pairs={{4,0},{8,4},{12,8},{16,12},{20,16},{24,20},{28,24},{5,1},{9,5},{13... | collective-permute-start | bytes 98312 | tf_op jit(solution)/shard_map/ppermute | solution.py:12
  104.7 10.5 %all-to-all-start = ((f32[8,3,4,256]{3,0,1,2:T(8,128)}), f32[8,3,4,256]{3,0,1,2:T(8,128)S(1)}, u32[]{:S(2)}, u32[]{:S(2)}) async-start(f32[8,3,4,256]{3,0,1,2:T(8,128)} %pad_maximum_fusion), calls=%async_computation | async-start | bytes 196608 | tf_op jit(solution)/shard_map/all_to_all | solution.py:16
  142.0 9.1 %all-to-all-start.1 = ((f32[8,3,4,256]{3,0,1,2:T(8,128)}), f32[8,3,4,256]{3,0,1,2:T(8,128)S(1)}, u32[]{:S(2)}, u32[]{:S(2)}) async-start(f32[8,3,4,256]{3,0,1,2:T(8,128)} %copy.49), calls=%async_computation.1 | async-start | bytes 196608 | tf_op jit(solution)/shard_map/all_to_all | solution.py:26
  151.1 4.6 %collective-permute-start.3 = (f32[8,4,256]{2,0,1:T(8,128)S(1)}, f32[8,4,256]{2,0,1:T(8,128)S(1)}, u32[]{:S(2)}, u32[]{:S(2)}) collective-permute-start(f32[8,4,256]{2,0,1:T(8,128)S(1)} %get-tuple-element.6), channel_id=1, source_target_pairs={{4,0},{8,4},{12,8},{16,12},{20,16},{24,20},{28,24},{5,1},{9,5},{13... | collective-permute-start | bytes 98312 | tf_op jit(solution)/shard_map/ppermute | solution.py:12
  153.7 6.1 %collective-permute-start.2 = (f32[8,4,256]{2,0,1:T(8,128)S(1)}, f32[8,4,256]{2,0,1:T(8,128)S(1)}, u32[]{:S(2)}, u32[]{:S(2)}) collective-permute-start(f32[8,4,256]{2,0,1:T(8,128)S(1)} %get-tuple-element.5), channel_id=1, source_target_pairs={{0,4},{4,8},{8,12},{12,16},{16,20},{20,24},{24,28},{1,5},{5,9},{9,... | collective-permute-start | bytes 98312 | tf_op jit(solution)/shard_map/ppermute | solution.py:12
where the time goes:
time: 232 us
  other arithmetic  134 us (58%)
  local copies, waits for them, and re-layouts  62.3 us (27%)
  starting transfers between devices  20.5 us (9%)
  waiting for transfers between devices  14.9 us (6%)
    scatter-add x1, other arithmetic, on_device(): jnp.zeros((fields, LOCAL), jnp.float32).at[:, local_map].add(element_values)  76.8 us
    gather x1, local copies, waits for them, and re-layouts, on_device(): return jnp.take(combined, local_map, axis=1)  28.6 us
    scatter-add x1, other arithmetic, on_device(): combined = assembled.at[:, send_node[0]].add(change)  20.2 us
    scatter-add x1, other arithmetic, on_device(): jnp.zeros((fields, owned_count), jnp.float32).at[:, targets].add(incoming)  17 us
    select_n x2, other arithmetic, on_device(): return jnp.take(combined, local_map, axis=1)  12.5 us
    gather x2, local copies, waits for them, and re-layouts, on_device(): jnp.take(assembled, send_node[0], axis=1)  11.1 us
    ppermute x4, starting transfers between devices, shifted(): return lax.ppermute(block, axis, route)  11 us
    gather x2, local copies, waits for them, and re-layouts, on_device(): jnp.take(totals, targets, axis=1).reshape(fields, 3, loc_count, slot_count)  8.56 us
  transfers between devices with their start and end apart: 6, of which 4 were waited for; matrix products, arithmetic and copies ran while one was open for 0% of the time, Pallas kernels for 0%

commit v1 on v0

--- a/solution.py
+++ b/solution.py
@@ -1,6 +1,8 @@
 import jax
 import jax.numpy as jnp
 from jax import lax
+from jax.experimental import pallas as pl
+from jax.experimental.pallas import tpu as pltpu
 from jax.sharding import PartitionSpec as P
 
 LOCAL = 10648
@@ -32,25 +34,94 @@
     return jnp.stack([lower, buffer[:, 1], upper], axis=1)
 
 
+BATCH = 32
+ROWS = 10656
+
+
+def add_rows(index_ref, value_ref, table_ref):
+    def step(b, carry):
+        base = pl.multiple_of(b * BATCH, BATCH)
+        nodes = [index_ref[base + k] for k in range(BATCH)]
+        held = [table_ref[pl.ds(n, 1), :] for n in nodes]
+        sums = [held[k] + value_ref[pl.ds(base + k, 1), :] for k in range(BATCH)]
+        for k in range(BATCH):
+            table_ref[pl.ds(nodes[k], 1), :] = sums[k]
+        return carry
+
+    lax.fori_loop(0, index_ref.shape[0] // BATCH, step, 0)
+
+
+def take_rows(index_ref, table_ref, out_ref):
+    def step(b, carry):
+        base = pl.multiple_of(b * BATCH, BATCH)
+        rows = [table_ref[pl.ds(index_ref[base + k], 1), :] for k in range(BATCH)]
+        for k in range(BATCH):
+            out_ref[pl.ds(base + k, 1), :] = rows[k]
+        return carry
+
+    lax.fori_loop(0, index_ref.shape[0] // BATCH, step, 0)
+
+
+def assemble_kernel(map_ref, send_ref, value_ref, table_ref, picked_ref):
+    chunk = 288
+
+    def clear(b, carry):
+        table_ref[pl.ds(pl.multiple_of(b * chunk, chunk), chunk), :] = jnp.zeros((chunk, table_ref.shape[1]), jnp.float32)
+        return carry
+
+    lax.fori_loop(0, ROWS // chunk, clear, 0)
+    add_rows(map_ref, value_ref, table_ref)
+    take_rows(send_ref, table_ref, picked_ref)
+
+
+def finish_kernel(map_ref, send_ref, change_ref, table_in, out_ref, table_ref):
+    pltpu.sync_copy(table_in, table_ref)
+    add_rows(send_ref, change_ref, table_ref)
+    take_rows(map_ref, table_ref, out_ref)
+
+
+SMEM = pl.BlockSpec(memory_space=pltpu.SMEM)
+VMEM = pl.BlockSpec(memory_space=pltpu.VMEM)
+
+
 def on_device(element_values, local_map, send_node, send_count, recv_slot):
-    fields = element_values.shape[0]
+    fields, span = element_values.shape
     loc_count = lax.axis_size("loc")
-    slot_count = send_node.shape[1] // (3 * loc_count)
+    slots_all = send_node.shape[1]
+    slot_count = slots_all // (3 * loc_count)
     owned_count = 2 * slot_count
-    assembled = jnp.zeros((fields, LOCAL), jnp.float32).at[:, local_map].add(element_values)
+    params = pltpu.CompilerParams(vmem_limit_bytes=48 * 1024 * 1024)
+    table, picked_rows = pl.pallas_call(
+        assemble_kernel,
+        out_shape=(
+            jax.ShapeDtypeStruct((ROWS, fields), jnp.float32),
+            jax.ShapeDtypeStruct((slots_all, fields), jnp.float32),
+        ),
+        in_specs=[SMEM, SMEM, VMEM],
+        out_specs=(VMEM, VMEM),
+        compiler_params=params,
+    )(local_map, send_node[0], element_values.T)
     live_slot = (jnp.arange(slot_count)[None, :] < send_count[0][:, None]).reshape(-1)
-    picked = jnp.where(live_slot[None, :], jnp.take(assembled, send_node[0], axis=1), 0.0)
+    picked = jnp.where(live_slot[None, :], picked_rows.T, 0.0)
     outgoing = picked.reshape(fields, 3, loc_count, slot_count)
     arrived = within_inward(across_inward(outgoing))
     incoming = arrived.reshape(fields, -1)
     targets = recv_slot[0]
-    totals = jnp.zeros((fields, owned_count), jnp.float32).at[:, targets].add(incoming)
-    replies = jnp.take(totals, targets, axis=1).reshape(fields, 3, loc_count, slot_count)
+    totals = jnp.zeros((fields, owned_count), jnp.float32).at[:, targets].add(incoming, mode="promise_in_bounds")
+    replies = totals.at[:, targets].get(mode="promise_in_bounds").reshape(fields, 3, loc_count, slot_count)
     homeward = across_outward(within_outward(replies))
     returned = homeward.reshape(fields, -1)
     change = jnp.where(live_slot[None, :], returned - picked, 0.0)
-    combined = assembled.at[:, send_node[0]].add(change)
-    return jnp.take(combined, local_map, axis=1)
+    spots = jnp.where(live_slot, send_node[0], LOCAL)
+    summed = pl.pallas_call(
+        finish_kernel,
+        out_shape=jax.ShapeDtypeStruct((span, fields), jnp.float32),
+        in_specs=[SMEM, SMEM, VMEM, pl.BlockSpec(memory_space=pl.ANY)],
+        out_specs=VMEM,
+        scratch_shapes=[pltpu.VMEM((ROWS, fields), jnp.float32)],
+        compiler_params=params,
+    )(local_map, spots, change.T, table)
+    return summed.T
 
 
 def solution(mesh):

time: 232 us -> 141 us (0.61)
  other arithmetic: 134 us -> 20.6 us
  Pallas kernels: 0 us -> 61.8 us
  local copies, waits for them, and re-layouts: 62.3 us -> 21.4 us
  blocking collectives: 0 us -> 8.5 us
  waiting for transfers between devices: 14.9 us -> 8.08 us
    scatter-add x3 -> x1, other arithmetic: 114 us -> 17 us  [on_device(): jnp.zeros((fields, owned_count), jnp.float32).at[:, targets]]
    pallas_call x0 -> x2, Pallas kernels: none -> 61.8 us  [the longest x1 36 us: on_device(): pl.pallas_call(assemble_kernel, out_shape=(jax.ShapeDtypeStruct((ROWS, fi...]
    gather x5 -> x1, local copies, waits for them, and re-layouts: 48.3 us -> 8.13 us  [on_device(): totals.at[:, targets].get(mode='promise_in_bounds')]
    select_n x6 -> x3, other arithmetic: 12.5 us -> 1.59 us  [the longest x1 1.57 us: on_device(): picked = jnp.where(live_slot[None, :], picked_rows.T, 0.0)]
    all_to_all x0 -> x1, blocking collectives: none -> 8.5 us  [within_outward(): lax.all_to_all(buffer, 'loc', split_axis=2, concat_axis=2, tiled=True)]
    select_n x2 -> x0, local copies, waits for them, and re-layouts: 6.05 us -> none  [the longest x1 5.4 us: on_device(): return jnp.take(combined, local_map, axis=1)]
    transpose x0 -> x1, local copies, waits for them, and re-layouts: none -> 5.4 us  [on_device(): return summed.T]
    all_to_all x1 -> x0, waiting for transfers between devices: 4.89 us -> none  [within_outward(): lax.all_to_all(buffer, 'loc', split_axis=2, concat_axis=2, tiled=True)]
  transfers between devices with their start and end apart: 6 -> 5, of which waited for: 4 -> 3; matrix products, arithmetic and copies ran while one was open for 0% -> 0% of each run, Pallas kernels for 0% -> 0%
where the time goes in v1:
time: 141 us; the launch traced here: 139 us
  Pallas kernels  61.8 us (44%)
  local copies, waits for them, and re-layouts  21.4 us (15%)
  other arithmetic  20.6 us (15%)
  starting transfers between devices  18.2 us (13%)
  blocking collectives  8.5 us (6%)
  waiting for transfers between devices  8.08 us (6%)
    pallas_call x1, Pallas kernels, on_device(): pl.pallas_call(assemble_kernel, out_shape=(jax.ShapeDtypeStruct((ROWS, fi...  36 us
    pallas_call x1, Pallas kernels, on_device(): pl.pallas_call(finish_kernel, out_shape=jax.ShapeDtypeStruct((span, field...  25.7 us
    scatter-add x1, other arithmetic, on_device(): jnp.zeros((fields, owned_count), jnp.float32).at[:, targets]  17 us
    ppermute x4, starting transfers between devices, shifted(): return lax.ppermute(block, axis, route)  12.9 us
    all_to_all x1, blocking collectives, within_outward(): lax.all_to_all(buffer, 'loc', split_axis=2, concat_axis=2, tiled=True)  8.5 us
    gather x1, local copies, waits for them, and re-layouts, on_device(): totals.at[:, targets].get(mode='promise_in_bounds')  8.13 us
    unnamed x12, local copies, waits for them, and re-layouts  5.65 us
    transpose x1, local copies, waits for them, and re-layouts, on_device(): return summed.T  5.4 us
  transfers between devices with their start and end apart: 5, of which 3 were waited for; matrix products, arithmetic and copies ran while one was open for 0% of the time, Pallas kernels for 0%

profile of v1, /device:TPU:12, one launch (start us, length us, event | category | flops | bytes accessed | tf_op | source)
XLA Modules:
  0.0 138.7 jit_solution(14062402565776738454)
XLA Ops:
  0.0 5.1 %copy.30 = f32[8,13824]{0,1:T(8,128)} copy(f32[8,13824]{1,0:T(8,128)} %param.5) | data formatting | bytes 884736 | tf_op args[0]
  5.2 0.0 copy-done.3
  5.2 0.1 iota_compare_fusion
  5.3 0.0 copy-done.1
  5.3 36.0 %shard_map.55 = (f32[10656,8]{1,0:T(8,128)}, f32[3072,8]{1,0:T(8,128)S(1)}) custom-call(s32[13824]{0:T(1024)S(1)} %copy-done, s32[3072]{0:T(1024)S(1)} %bitcast.35, f32[13824,8]{1,0:T(8,128)} %bitcast.37), custom_call_target="tpu_custom_call" | custom-call | tf_op jit(solution)/shard_map/pallas_call | solution.py:94
  41.3 1.6 %broadcast_select_fusion = f32[3072,8]{1,0:T(8,128)S(1)} fusion(f32[3072,8]{1,0:T(8,128)S(1)} %get-tuple-element.7, pred[3072]{0:T(1024)(128)(4,1)S(1)} %lt.38), kind=kLoop, calls=%fused_computation.4 | loop fusion | flops 24576 | bytes 199680 | tf_op jit(solution)/shard_map/jit(_where)/select_n | solution.py:105
  42.9 0.0 copy-start.2
  42.9 0.1 fusion.3
  43.0 0.2 copy.44
  43.1 1.9 %collective-permute-start.1 = (f32[8,4,256]{2,0,1:T(8,128)S(1)}, f32[8,4,256]{2,0,1:T(8,128)S(1)}, u32[]{:S(2)}, u32[]{:S(2)}) collective-permute-start(f32[8,4,256]{2,0,1:T(8,128)S(1)} %bitcast.44), channel_id=1, source_target_pairs={{0,4},{4,8},{8,12},{12,16},{16,20},{20,24},{24,28},{1,5},{5,9},{9,... | collective-permute-start | bytes 98312 | tf_op jit(solution)/shard_map/ppermute | solution.py:14
  45.1 0.2 copy.42
  45.2 4.5 %collective-permute-start = (f32[8,4,256]{2,0,1:T(8,128)S(1)}, f32[8,4,256]{2,0,1:T(8,128)S(1)}, u32[]{:S(2)}, u32[]{:S(2)}) collective-permute-start(f32[8,4,256]{2,0,1:T(8,128)S(1)} %bitcast.45), channel_id=1, source_target_pairs={{4,0},{8,4},{12,8},{16,12},{20,16},{24,20},{28,24},{5,1},{9,5},{13... | collective-permute-start | bytes 98312 | tf_op jit(solution)/shard_map/ppermute | solution.py:14
  49.8 0.2 copy.43
  50.0 0.0 collective-permute-done.1
  50.0 1.4 collective-permute-done
  51.4 0.6 copy.34
  52.0 5.3 %all-to-all-start = ((f32[8,3,4,256]{3,0,1,2:T(8,128)}), f32[8,3,4,256]{3,0,1,2:T(8,128)S(1)}, u32[]{:S(2)}, u32[]{:S(2)}) async-start(f32[8,3,4,256]{3,0,1,2:T(8,128)} %copy.34), calls=%async_computation | async-start | bytes 196608 | tf_op jit(solution)/shard_map/all_to_all | solution.py:18
  57.3 5.1 %all-to-all-done = f32[8,3,4,256]{3,0,1,2:T(8,128)S(1)} async-done(((f32[8,3,4,256]{3,0,1,2:T(8,128)}), f32[8,3,4,256]{3,0,1,2:T(8,128)S(1)}, u32[]{:S(2)}, u32[]{:S(2)}) %all-to-all-start) | async-done | bytes 98336 | tf_op jit(solution)/shard_map/all_to_all | solution.py:18
  62.5 0.1 reshape.71
  62.6 0.5 copy.36
  63.0 17.0 %scatter_custom_fusion = f32[8,512]{0,1:T(8,128)S(1)} fusion(s32[3072]{0:T(1024)S(1)} %bitcast.43, f32[3072,8]{1,0:T(8,128)S(1)} %copy.36, f32[]{:T(128)} %constant.0.clone.1), kind=kCustom, calls=%fused_computation.5 | custom fusion | flops 24576 | bytes 16388 | tf_op jit(solution)/shard_map/scatter-add | solution.py:110
  80.0 8.1 %gather_fusion = f32[3072,8]{1,0:T(8,128)S(1)} fusion(f32[8,512]{0,1:T(8,128)S(1)} %scatter_custom_fusion, s32[3072]{0:T(1024)S(1)} %broadcast_clamp_fusion), kind=kCustom, calls=%fused_computation | custom fusion | bytes 208896 | tf_op jit(solution)/shard_map/gather | solution.py:111
  88.2 0.4 copy.37
  88.6 8.5 %all_to_all.10 = f32[8,3,4,256]{3,0,1,2:T(8,128)S(1)} all-to-all(f32[8,3,4,256]{3,0,1,2:T(8,128)S(1)} %copy.37), channel_id=1, replica_groups=mesh['grp'=8,'loc'=4] {'loc'}, dimensions={2} | all-to-all | bytes 196608 | tf_op jit(solution)/shard_map/all_to_all | solution.py:28
  97.1 1.9 %collective-permute-start.2 = (f32[8,4,256]{2,0,1:T(8,128)S(1)}, f32[8,4,256]{2,0,1:T(8,128)S(1)}, u32[]{:S(2)}, u32[]{:S(2)}) collective-permute-start(f32[8,4,256]{2,0,1:T(8,128)S(1)} %get-tuple-element.12), channel_id=1, source_target_pairs={{0,4},{4,8},{8,12},{12,16},{16,20},{20,24},{24,28},{1,5},{5,9},{9,... | collective-permute-start | bytes 98312 | tf_op jit(solution)/shard_map/ppermute | solution.py:14
  99.0 4.5 %collective-permute-start.3 = (f32[8,4,256]{2,0,1:T(8,128)S(1)}, f32[8,4,256]{2,0,1:T(8,128)S(1)}, u32[]{:S(2)}, u32[]{:S(2)}) collective-permute-start(f32[8,4,256]{2,0,1:T(8,128)S(1)} %get-tuple-element.13), channel_id=1, source_target_pairs={{4,0},{8,4},{12,8},{16,12},{20,16},{24,20},{28,24},{5,1},{9,5},{13... | collective-permute-start | bytes 98312 | tf_op jit(solution)/shard_map/ppermute | solution.py:14
  103.6 0.0 collective-permute-done.2
  103.6 1.6 %collective-permute-done.3 = f32[8,4,256]{2,0,1:T(8,128)S(1)} collective-permute-done((f32[8,4,256]{2,0,1:T(8,128)S(1)}, f32[8,4,256]{2,0,1:T(8,128)S(1)}, u32[]{:S(2)}, u32[]{:S(2)}) %collective-permute-start.3) | collective-permute-done | bytes 32800 | tf_op jit(solution)/shard_map/ppermute | solution.py:14
  105.2 0.5 copy.40
  105.6 2.0 %fusion = f32[8,3072]{0,1:T(8,128)S(1)} fusion(f32[8,3,4,256]{0,3,2,1:T(8,128)S(1)} %copy.40, pred[3072]{0:T(1024)(128)(4,1)S(1)} %lt.38, f32[3072,8]{1,0:T(8,128)S(1)} %get-tuple-element.7), kind=kLoop, calls=%fused_computation.3 | loop fusion | flops 73728 | bytes 297984 | tf_op jit(solution)/shard_map/jit(_where)/select_n | solution.py:114
  107.6 25.7 %shard_map.56 = f32[13824,8]{1,0:T(8,128)} custom-call(s32[13824]{0:T(1024)S(1)} %copy-done, s32[3072]{0:T(1024)S(1)} %broadcast_select_fusion.1.send_ref, f32[3072,8]{1,0:T(8,128)S(1)} %bitcast.34, f32[10656,8]{1,0:T(8,128)} %get-tuple-element.8.table_in), custom_call_target="tpu_custom_call" | custom-call | tf_op jit(solution)/shard_map/pallas_call | solution.py:116
  133.3 5.4 %copy.41 = f32[8,13824]{1,0:T(8,128)} copy(f32[8,13824]{0,1:T(8,128)} %bitcast.38) | data formatting | bytes 884736 | tf_op jit(solution)/shard_map/transpose | solution.py:124
  (13 shorter events, 0.1 us)
Async XLA Ops:
  0.0 5.2 %copy-start.3 = (s32[1,12]{1,0:T(1,128)S(1)}, s32[1,12]{1,0:T(1,128)}, u32[]{:S(2)}) copy-start(s32[1,12]{1,0:T(1,128)} %param.8) | copy-start | bytes 148
  0.0 5.3 %copy-start.1 = (s32[1,3072]{1,0:T(1,128)S(1)}, s32[1,3072]{1,0:T(1,128)}, u32[]{:S(2)}) copy-start(s32[1,3072]{1,0:T(1,128)} %param.7) | copy-start | bytes 36868
  0.0 5.3 %copy-start = (s32[13824]{0:T(1024)S(1)}, s32[13824]{0:T(1024)}, u32[]{:S(2)}) copy-start(s32[13824]{0:T(1024)} %map_ref.3) | copy-start | bytes 165892
  42.9 6.9 %copy-start.2 = (s32[1,3072]{1,0:T(1,128)S(1)}, s32[1,3072]{1,0:T(1,128)}, u32[]{:S(2)}) copy-start(s32[1,3072]{1,0:T(1,128)} %param.9) | copy-start | bytes 36868
  43.1 6.8 %collective-permute-start.1 = (f32[8,4,256]{2,0,1:T(8,128)S(1)}, f32[8,4,256]{2,0,1:T(8,128)S(1)}, u32[]{:S(2)}, u32[]{:S(2)}) collective-permute-start(f32[8,4,256]{2,0,1:T(8,128)S(1)} %bitcast.44), channel_id=1, source_target_pairs={{0,4},{4,8},{8,12},{12,16},{16,20},{20,24},{24,28},{1,5},{5,9},{9,... | collective-permute-start | bytes 98312 | tf_op jit(solution)/shard_map/ppermute | solution.py:14
  45.2 6.1 %collective-permute-start = (f32[8,4,256]{2,0,1:T(8,128)S(1)}, f32[8,4,256]{2,0,1:T(8,128)S(1)}, u32[]{:S(2)}, u32[]{:S(2)}) collective-permute-start(f32[8,4,256]{2,0,1:T(8,128)S(1)} %bitcast.45), channel_id=1, source_target_pairs={{4,0},{8,4},{12,8},{16,12},{20,16},{24,20},{28,24},{5,1},{9,5},{13... | collective-permute-start | bytes 98312 | tf_op jit(solution)/shard_map/ppermute | solution.py:14
  52.0 10.5 %all-to-all-start = ((f32[8,3,4,256]{3,0,1,2:T(8,128)}), f32[8,3,4,256]{3,0,1,2:T(8,128)S(1)}, u32[]{:S(2)}, u32[]{:S(2)}) async-start(f32[8,3,4,256]{3,0,1,2:T(8,128)} %copy.34), calls=%async_computation | async-start | bytes 196608 | tf_op jit(solution)/shard_map/all_to_all | solution.py:18
  97.1 6.5 %collective-permute-start.2 = (f32[8,4,256]{2,0,1:T(8,128)S(1)}, f32[8,4,256]{2,0,1:T(8,128)S(1)}, u32[]{:S(2)}, u32[]{:S(2)}) collective-permute-start(f32[8,4,256]{2,0,1:T(8,128)S(1)} %get-tuple-element.12), channel_id=1, source_target_pairs={{0,4},{4,8},{8,12},{12,16},{16,20},{20,24},{24,28},{1,5},{5,9},{9,... | collective-permute-start | bytes 98312 | tf_op jit(solution)/shard_map/ppermute | solution.py:14
  99.0 6.1 %collective-permute-start.3 = (f32[8,4,256]{2,0,1:T(8,128)S(1)}, f32[8,4,256]{2,0,1:T(8,128)S(1)}, u32[]{:S(2)}, u32[]{:S(2)}) collective-permute-start(f32[8,4,256]{2,0,1:T(8,128)S(1)} %get-tuple-element.13), channel_id=1, source_target_pairs={{4,0},{8,4},{12,8},{16,12},{20,16},{24,20},{28,24},{5,1},{9,5},{13... | collective-permute-start | bytes 98312 | tf_op jit(solution)/shard_map/ppermute | solution.py:14
